TPU v7x, 512 devices: a whole 4x8x8 slice. The times are simulated.
512 devices in a mesh: mem: 32 (over z, y_hi, core), gy: 4 (over y_lo), gx: 4 (over x).
Axes of the slice: x: 4, y: 8 (y_hi: 2, y_lo: 4; y = y_hi * 4 + y_lo), z: 8, core: 2. Of those that a mesh axis runs over, the one named last changes fastest.
Arguments:
- increment: float32 [4, 256, 4096], P(None, 'gy', 'gx'), may hold values from -6 to 6
- members: float32 [32, 4, 256, 4096], P('mem', None, 'gy', 'gx'), may hold values from -6 to 6
- zonal_diff: float32 [256, 4096], P('gy', 'gx'), may hold values from 0.05 to 0.35
- merid_diff: float32 [256, 4096], P('gy', 'gx'), may hold values from 0.02 to 0.15
- sea_mask: int32 [256, 4096], P('gy', 'gx'), may hold values 0 or 1
Outputs:
- product: float32 [4, 256, 4096], P(None, 'gy', 'gx')
All inputs are finite; a program needn't handle non-finite values. No bound on the sum of `sea_mask` on one device may be relied on, other than what follows from the above.
Results may differ from a plain program's by a relative error of at most 0.00002.
Values sent between devices are 32-bit elements; how exact they have to be, the bound alone decides.
A program may use at most 64 MiB of HBM per device.

v0:
```python
import jax
import jax.numpy as jnp
from jax import lax
from jax.sharding import PartitionSpec as P

STEPS = 4


def extended(shard, sides, width, wrap):
    for axis, dim in sides:
        size, length = (lax.axis_size(axis), shard.shape[dim])
        up = [(i, (i + 1) % size) for i in range(size if wrap else size - 1)]
        down = [(j, i) for i, j in up]
        last = lax.slice_in_dim(shard, length - width, length, axis=dim)
        initial = lax.slice_in_dim(shard, 0, width, axis=dim)
        before = lax.ppermute(last, axis, up)
        after = lax.ppermute(initial, axis, down)
        shard = jnp.concatenate([before, shard, after], axis=dim)
    return shard


def face_weights(zonal, merid, wet):
    east = zonal[:, :-1] * wet[:, :-1] * wet[:, 1:]
    north = merid[:-1, :] * wet[:-1, :] * wet[1:, :]
    return (east, north)


def sweep(field, east, north):
    centre = field[:, 1:-1, 1:-1]
    go_east = east[1:-1, 1:] * (field[:, 1:-1, 2:] - centre)
    go_west = east[1:-1, :-1] * (centre - field[:, 1:-1, :-2])
    go_north = north[1:, 1:-1] * (field[:, 2:, 1:-1] - centre)
    go_south = north[:-1, 1:-1] * (centre - field[:, :-2, 1:-1])
    return centre + go_east - go_west + go_north - go_south


def trimmed(table, margin):
    return table[margin : table.shape[0] - margin, margin : table.shape[1] - margin]


def shards(increment, members, zonal_diff, merid_diff, sea_mask):
    member = members[0]
    wet = sea_mask.astype(jnp.float32)
    field = member * increment * wet
    stacked = jnp.stack([zonal_diff, merid_diff, wet])
    stacked = extended(stacked, (("gy", 1),), STEPS, False)
    stacked = extended(stacked, (("gx", 2),), STEPS, True)
    east, north = face_weights(stacked[0], stacked[1], stacked[2])
    near_east = trimmed(east, STEPS - 1)
    near_north = trimmed(north, STEPS - 1)
    first = 0
    for step in range(first, STEPS):
        padded = extended(field, (("gy", 1),), 1, False)
        padded = extended(padded, (("gx", 2),), 1, True)
        field = sweep(padded, near_east, near_north)
    term = member * field
    return lax.psum(term, "mem")


def solution(mesh):
    return jax.shard_map(
        shards,
        mesh=mesh,
        in_specs=(
            P(None, "gy", "gx"),
            P("mem", None, "gy", "gx"),
            P("gy", "gx"),
            P("gy", "gx"),
            P("gy", "gx"),
        ),
        out_specs=P(None, "gy", "gx"),
        check_vma=False,
    )
```

profile of v0, /device:TPU:1, one launch (start us, length us, event | category | flops | bytes accessed | tf_op | source)
XLA Modules:
  0.0 460.9 jit_solution(7152213403313559908)
XLA Ops:
  6.5 1.1 convert_bitcast_fusion
  7.7 4.0 collective-permute-start
  11.8 1.3 collective-permute-start.1
  13.1 1.4 fusion.49
  14.5 1.3 collective-permute-start.5
  15.8 4.6 %collective-permute-start.4 = (f32[4,1,1024]{2,1,0:T(1,128)S(1)}, f32[4,1,1024]{2,1,0:T(1,128)S(1)}, u32[]{:S(2)}, u32[]{:S(2)}) collective-permute-start(f32[4,1,1024]{2,1,0:T(1,128)S(1)} %get-tuple-element.20), channel_id=1, source_target_pairs={{0,4},{4,8},{8,12},{1,5},{5,9},{9,13},{2,6},{6,10},{10,14},{3,7},{... | collective-permute-start | bytes 49160 | tf_op jit(solution)/shard_map/ppermute | solution.py:16
  20.7 4.4 collective-permute-start.3
  25.1 1.9 collective-permute-start.2
  27.2 4.6 collective-permute-start.6
  31.7 1.9 collective-permute-start.7
  34.3 1.4 concatenate.71
  36.4 2.5 collective-permute-done.7
  39.0 1.7 fusion.39
  40.7 1.3 collective-permute-start.9
  42.0 4.0 collective-permute-start.8
  46.0 0.8 collective-permute-done.8
  47.0 2.1 collective-permute-start.10
  49.1 3.2 collective-permute-start.11
  52.9 3.3 collective-permute-done.11
  57.1 1.3 collective-permute-start.13
  58.4 4.3 collective-permute-start.12
  63.6 1.9 collective-permute-start.14
  65.5 3.4 collective-permute-start.15
  69.5 3.1 collective-permute-done.15
  73.5 1.4 collective-permute-start.17
  74.9 4.3 collective-permute-start.16
  80.2 1.9 collective-permute-start.18
  82.1 3.4 collective-permute-start.19
  86.1 3.1 collective-permute-done.19
  89.2 1.8 fusion.3
  91.1 360.7 %all-reduce.2.cloned.1.call-done = f32[4,64,1024]{2,1,0:T(8,128)} async-done(((f32[4,64,1024]{2,1,0:T(8,128)}), f32[4,64,1024]{2,1,0:T(8,128)}) %all-reduce.2.cloned.1.call-update) | async-done | bytes 1048592 | tf_op jit(solution)/shard_map/psum | solution.py:57
  451.7 2.3 copy.7
  (44 shorter events, 7.3 us)
Async XLA Ops:
  6.5 1.1 copy-start.2
  6.5 1.1 copy-start.3
  6.5 6.5 %copy-start = (f32[1,4,64,1024]{3,2,1,0:T(8,128)S(1)}, f32[1,4,64,1024]{3,2,1,0:T(8,128)}, u32[]{:S(2)}) copy-start(f32[1,4,64,1024]{3,2,1,0:T(8,128)} %param.6) | copy-start | bytes 3145732
  6.5 445.2 %all-reduce.2.cloned.1.call-start = ((), (), s32[]{:S(2)}) async-start(), calls=%async_computation | async-start | bytes 2097152 | tf_op jit(solution)/shard_map/psum | solution.py:57
  7.7 12.7 %collective-permute-start = (f32[3,4,1024]{2,1,0:T(4,128)S(1)}, f32[3,4,1024]{2,1,0:T(4,128)S(1)}, u32[]{:S(2)}, u32[]{:S(2)}) collective-permute-start(f32[3,4,1024]{2,1,0:T(4,128)S(1)} %get-tuple-element.25), channel_id=1, source_target_pairs={{0,4},{4,8},{8,12},{1,5},{5,9},{9,13},{2,6},{6,10},{10,14},{3,7},{... | collective-permute-start | bytes 147464 | tf_op jit(solution)/shard_map/ppermute | solution.py:16
  11.8 8.7 %collective-permute-start.1 = (f32[3,4,1024]{2,1,0:T(4,128)S(1)}, f32[3,4,1024]{2,1,0:T(4,128)S(1)}, u32[]{:S(2)}, u32[]{:S(2)}) collective-permute-start(f32[3,4,1024]{2,1,0:T(4,128)S(1)} %get-tuple-element.26), channel_id=1, source_target_pairs={{4,0},{8,4},{12,8},{5,1},{9,5},{13,9},{6,2},{10,6},{14,10},{7,3},{... | collective-permute-start | bytes 147464 | tf_op jit(solution)/shard_map/ppermute | solution.py:17
  14.5 12.5 %collective-permute-start.5 = (f32[4,1,1024]{2,1,0:T(1,128)S(1)}, f32[4,1,1024]{2,1,0:T(1,128)S(1)}, u32[]{:S(2)}, u32[]{:S(2)}) collective-permute-start(f32[4,1,1024]{2,1,0:T(1,128)S(1)} %get-tuple-element.19), channel_id=1, source_target_pairs={{4,0},{8,4},{12,8},{5,1},{9,5},{13,9},{6,2},{10,6},{14,10},{7,3},{... | collective-permute-start | bytes 49160 | tf_op jit(solution)/shard_map/ppermute | solution.py:17
  15.8 11.2 %collective-permute-start.4 = (f32[4,1,1024]{2,1,0:T(1,128)S(1)}, f32[4,1,1024]{2,1,0:T(1,128)S(1)}, u32[]{:S(2)}, u32[]{:S(2)}) collective-permute-start(f32[4,1,1024]{2,1,0:T(1,128)S(1)} %get-tuple-element.20), channel_id=1, source_target_pairs={{0,4},{4,8},{8,12},{1,5},{5,9},{9,13},{2,6},{6,10},{10,14},{3,7},{... | collective-permute-start | bytes 49160 | tf_op jit(solution)/shard_map/ppermute | solution.py:16
  20.7 13.0 %collective-permute-start.3 = (f32[3,72,4]{2,1,0:T(8,128)S(1)}, f32[3,72,4]{2,1,0:T(8,128)S(1)}, u32[]{:S(2)}, u32[]{:S(2)}) collective-permute-start(f32[3,72,4]{2,1,0:T(8,128)S(1)} %get-tuple-element.23), channel_id=1, source_target_pairs={{1,0},{2,1},{3,2},{0,3},{5,4},{6,5},{7,6},{4,7},{9,8},{10,9},{11,1... | collective-permute-start | bytes 10376 | tf_op jit(solution)/shard_map/ppermute | solution.py:17
  25.1 9.2 %collective-permute-start.2 = (f32[3,72,4]{2,1,0:T(8,128)S(1)}, f32[3,72,4]{2,1,0:T(8,128)}, u32[]{:S(2)}, u32[]{:S(2)}) collective-permute-start(f32[3,72,4]{2,1,0:T(8,128)S(1)} %get-tuple-element.24), channel_id=1, source_target_pairs={{0,1},{1,2},{2,3},{3,0},{4,5},{5,6},{6,7},{7,4},{8,9},{9,10},{10,1... | collective-permute-start | bytes 10376 | tf_op jit(solution)/shard_map/ppermute | solution.py:16
  27.2 9.3 %collective-permute-start.6 = (f32[4,66,1]{2,1,0:T(8,128)S(1)}, f32[4,66,1]{2,1,0:T(8,128)S(1)}, u32[]{:S(2)}, u32[]{:S(2)}) collective-permute-start(f32[4,66,1]{2,1,0:T(8,128)S(1)} %get-tuple-element.11), channel_id=1, source_target_pairs={{1,0},{2,1},{3,2},{0,3},{5,4},{6,5},{7,6},{4,7},{9,8},{10,9},{11,1... | collective-permute-start | bytes 3176 | tf_op jit(solution)/shard_map/ppermute | solution.py:17
  31.7 7.2 %collective-permute-start.7 = (f32[4,66,1]{2,1,0:T(8,128)S(1)}, f32[4,66,1]{2,1,0:T(8,128)}, u32[]{:S(2)}, u32[]{:S(2)}) collective-permute-start(f32[4,66,1]{2,1,0:T(8,128)S(1)} %get-tuple-element.12), channel_id=1, source_target_pairs={{0,1},{1,2},{2,3},{3,0},{4,5},{5,6},{6,7},{7,4},{8,9},{9,10},{10,1... | collective-permute-start | bytes 3176 | tf_op jit(solution)/shard_map/ppermute | solution.py:16
  33.7 0.6 copy-start.4
  40.7 5.3 %collective-permute-start.9 = (f32[4,1,1024]{2,1,0:T(1,128)S(1)}, f32[4,1,1024]{2,1,0:T(1,128)S(1)}, u32[]{:S(2)}, u32[]{:S(2)}) collective-permute-start(f32[4,1,1024]{2,1,0:T(1,128)S(1)} %get-tuple-element.17), channel_id=1, source_target_pairs={{4,0},{8,4},{12,8},{5,1},{9,5},{13,9},{6,2},{10,6},{14,10},{7,3},{... | collective-permute-start | bytes 49160 | tf_op jit(solution)/shard_map/ppermute | solution.py:17
  42.0 4.8 %collective-permute-start.8 = (f32[4,1,1024]{2,1,0:T(1,128)S(1)}, f32[4,1,1024]{2,1,0:T(1,128)S(1)}, u32[]{:S(2)}, u32[]{:S(2)}) collective-permute-start(f32[4,1,1024]{2,1,0:T(1,128)S(1)} %get-tuple-element.18), channel_id=1, source_target_pairs={{0,4},{4,8},{8,12},{1,5},{5,9},{9,13},{2,6},{6,10},{10,14},{3,7},{... | collective-permute-start | bytes 49160 | tf_op jit(solution)/shard_map/ppermute | solution.py:16
  47.0 5.9 %collective-permute-start.10 = (f32[4,66,1]{2,1,0:T(8,128)S(1)}, f32[4,66,1]{2,1,0:T(8,128)S(1)}, u32[]{:S(2)}, u32[]{:S(2)}) collective-permute-start(f32[4,66,1]{2,1,0:T(8,128)S(1)} %get-tuple-element.9), channel_id=1, source_target_pairs={{1,0},{2,1},{3,2},{0,3},{5,4},{6,5},{7,6},{4,7},{9,8},{10,9},{11,1... | collective-permute-start | bytes 3176 | tf_op jit(solution)/shard_map/ppermute | solution.py:17
  49.1 7.1 %collective-permute-start.11 = (f32[4,66,1]{2,1,0:T(8,128)S(1)}, f32[4,66,1]{2,1,0:T(8,128)S(1)}, u32[]{:S(2)}, u32[]{:S(2)}) collective-permute-start(f32[4,66,1]{2,1,0:T(8,128)S(1)} %get-tuple-element.10), channel_id=1, source_target_pairs={{0,1},{1,2},{2,3},{3,0},{4,5},{5,6},{6,7},{7,4},{8,9},{9,10},{10,1... | collective-permute-start | bytes 3176 | tf_op jit(solution)/shard_map/ppermute | solution.py:16
  57.1 5.6 %collective-permute-start.13 = (f32[4,1,1024]{2,1,0:T(1,128)S(1)}, f32[4,1,1024]{2,1,0:T(1,128)S(1)}, u32[]{:S(2)}, u32[]{:S(2)}) collective-permute-start(f32[4,1,1024]{2,1,0:T(1,128)S(1)} %get-tuple-element.15), channel_id=1, source_target_pairs={{4,0},{8,4},{12,8},{5,1},{9,5},{13,9},{6,2},{10,6},{14,10},{7,3},{... | collective-permute-start | bytes 49160 | tf_op jit(solution)/shard_map/ppermute | solution.py:17
  58.4 5.1 %collective-permute-start.12 = (f32[4,1,1024]{2,1,0:T(1,128)S(1)}, f32[4,1,1024]{2,1,0:T(1,128)S(1)}, u32[]{:S(2)}, u32[]{:S(2)}) collective-permute-start(f32[4,1,1024]{2,1,0:T(1,128)S(1)} %get-tuple-element.16), channel_id=1, source_target_pairs={{0,4},{4,8},{8,12},{1,5},{5,9},{9,13},{2,6},{6,10},{10,14},{3,7},{... | collective-permute-start | bytes 49160 | tf_op jit(solution)/shard_map/ppermute | solution.py:16
  63.6 5.9 %collective-permute-start.14 = (f32[4,66,1]{2,1,0:T(8,128)S(1)}, f32[4,66,1]{2,1,0:T(8,128)S(1)}, u32[]{:S(2)}, u32[]{:S(2)}) collective-permute-start(f32[4,66,1]{2,1,0:T(8,128)S(1)} %get-tuple-element.7), channel_id=1, source_target_pairs={{1,0},{2,1},{3,2},{0,3},{5,4},{6,5},{7,6},{4,7},{9,8},{10,9},{11,1... | collective-permute-start | bytes 3176 | tf_op jit(solution)/shard_map/ppermute | solution.py:17
  65.5 7.1 %collective-permute-start.15 = (f32[4,66,1]{2,1,0:T(8,128)S(1)}, f32[4,66,1]{2,1,0:T(8,128)S(1)}, u32[]{:S(2)}, u32[]{:S(2)}) collective-permute-start(f32[4,66,1]{2,1,0:T(8,128)S(1)} %get-tuple-element.8), channel_id=1, source_target_pairs={{0,1},{1,2},{2,3},{3,0},{4,5},{5,6},{6,7},{7,4},{8,9},{9,10},{10,1... | collective-permute-start | bytes 3176 | tf_op jit(solution)/shard_map/ppermute | solution.py:16
  73.5 15.7 %copy-start.1 = (f32[1,4,64,1024]{3,2,1,0:T(8,128)S(1)}, f32[1,4,64,1024]{3,2,1,0:T(8,128)}, u32[]{:S(2)}) copy-start(f32[1,4,64,1024]{3,2,1,0:T(8,128)} %param.6) | copy-start | bytes 3145732
  73.5 5.7 %collective-permute-start.17 = (f32[4,1,1024]{2,1,0:T(1,128)S(1)}, f32[4,1,1024]{2,1,0:T(1,128)S(1)}, u32[]{:S(2)}, u32[]{:S(2)}) collective-permute-start(f32[4,1,1024]{2,1,0:T(1,128)S(1)} %get-tuple-element.13), channel_id=1, source_target_pairs={{4,0},{8,4},{12,8},{5,1},{9,5},{13,9},{6,2},{10,6},{14,10},{7,3},{... | collective-permute-start | bytes 49160 | tf_op jit(solution)/shard_map/ppermute | solution.py:17
  74.9 5.1 %collective-permute-start.16 = (f32[4,1,1024]{2,1,0:T(1,128)S(1)}, f32[4,1,1024]{2,1,0:T(1,128)S(1)}, u32[]{:S(2)}, u32[]{:S(2)}) collective-permute-start(f32[4,1,1024]{2,1,0:T(1,128)S(1)} %get-tuple-element.14), channel_id=1, source_target_pairs={{0,4},{4,8},{8,12},{1,5},{5,9},{9,13},{2,6},{6,10},{10,14},{3,7},{... | collective-permute-start | bytes 49160 | tf_op jit(solution)/shard_map/ppermute | solution.py:16
  80.2 5.9 %collective-permute-start.18 = (f32[4,66,1]{2,1,0:T(8,128)S(1)}, f32[4,66,1]{2,1,0:T(8,128)S(1)}, u32[]{:S(2)}, u32[]{:S(2)}) collective-permute-start(f32[4,66,1]{2,1,0:T(8,128)S(1)} %get-tuple-element.5), channel_id=1, source_target_pairs={{1,0},{2,1},{3,2},{0,3},{5,4},{6,5},{7,6},{4,7},{9,8},{10,9},{11,1... | collective-permute-start | bytes 3176 | tf_op jit(solution)/shard_map/ppermute | solution.py:17
  82.1 7.1 %collective-permute-start.19 = (f32[4,66,1]{2,1,0:T(8,128)S(1)}, f32[4,66,1]{2,1,0:T(8,128)S(1)}, u32[]{:S(2)}, u32[]{:S(2)}) collective-permute-start(f32[4,66,1]{2,1,0:T(8,128)S(1)} %get-tuple-element.6), channel_id=1, source_target_pairs={{0,1},{1,2},{2,3},{3,0},{4,5},{5,6},{6,7},{7,4},{8,9},{9,10},{10,1... | collective-permute-start | bytes 3176 | tf_op jit(solution)/shard_map/ppermute | solution.py:16
Sparse Core Ops, SparseCore 0:
  91.2 360.4 all-reduce.1
where the time goes:
time: 462 us; the launch traced here: 461 us
  waiting for transfers between devices  377 us (82%)
  starting transfers between devices  56.4 us (12%)
  between operations  13.8 us (3%)
  other arithmetic  8.6 us (2%)
  local copies, waits for them, and re-layouts  5.01 us (1%)
    psum x1, waiting for transfers between devices, shards(): return lax.psum(term, 'mem')  361 us
    ppermute x10, starting transfers between devices, extended(): before = lax.ppermute(last, axis, up)  34.9 us
    ppermute x10, starting transfers between devices, extended(): after = lax.ppermute(initial, axis, down)  21.5 us
    ppermute x10, waiting for transfers between devices, extended(): before = lax.ppermute(last, axis, up)  14.6 us
  transfers between devices with their start and end apart: 21, of which 11 were waited for; matrix products, arithmetic and copies ran while one was open for 1% of the time, Pallas kernels for 0%

commit v1 on v0

v1 whole, which is shorter than its diff:
```python
import jax
import jax.numpy as jnp
from jax import lax
from jax.experimental import pallas as pl
from jax.experimental.pallas import tpu as pltpu
from jax.sharding import PartitionSpec as P

STEPS = 4
LEVELS = 4
ROWS = 64
COLS = 1024
XROWS = ROWS + 8
XCOLS = COLS + 128
HALF = COLS // 2
MESH = pl.DeviceIdType.MESH
F32 = jnp.float32


def kernel(
    inc_hbm, mem_hbm, zon_hbm, mer_hbm, sea_hbm, out,
    inc, mem, zon, mer, sea,
    field, other, wet, east, north,
    rows_out, rows_in, cols_out, cols_in, corner_in,
    term, peer, part, gathered, mine, across,
    load_sem, halo_send, halo_recv, core_send, core_recv,
    red_send, red_recv, y_send, y_recv, ag_send, ag_recv, fwd_send, fwd_recv,
):
    me = lax.axis_index("mem")
    gy = lax.axis_index("gy")
    gx = lax.axis_index("gx")
    z = me // 4
    hi = lax.rem(me // 2, 2)
    core = lax.rem(me, 2)

    def member_at(z_, hi_, core_):
        return z_ * 4 + hi_ * 2 + core_

    def beside(dy, dx):
        y = lax.rem(hi * 4 + gy + dy + 8, 8)
        return (member_at(z, y // 4, core), lax.rem(y, 4), lax.rem(gx + dx + 4, 4))

    def along(k):
        return (member_at(lax.rem(z + k, 8), hi, core), gy, gx)

    core_peer = (member_at(z, hi, 1 - core), gy, gx)
    y_peer = (member_at(z, 1 - hi, core), gy, gx)

    barrier = pltpu.get_barrier_semaphore()
    around = [(-1, 0), (1, 0), (0, -1), (0, 1), (-1, -1), (1, -1), (-1, 1), (1, 1)]
    partners = [beside(dy, dx) for dy, dx in around]
    partners += [core_peer, y_peer] + [along(k) for k in range(1, 8)]
    for device in partners:
        pl.semaphore_signal(barrier, inc=1, device_id=device, device_id_type=MESH)

    loads = [
        pltpu.make_async_copy(sea_hbm, sea, load_sem.at[0]),
        pltpu.make_async_copy(zon_hbm, zon, load_sem.at[1]),
        pltpu.make_async_copy(mer_hbm, mer, load_sem.at[2]),
        pltpu.make_async_copy(inc_hbm, inc, load_sem.at[3]),
        pltpu.make_async_copy(mem_hbm.at[0], mem, load_sem.at[4]),
    ]
    for load in loads:
        load.start()
    for load in loads:
        load.wait()

    sub = lax.broadcasted_iota(jnp.int32, (8, 1), 0)
    low = sub < 4
    lane = lax.broadcasted_iota(jnp.int32, (1, 128), 1)

    def start_tile(r, carry):
        at = pl.ds(pl.multiple_of(r * 8, 8), 8)
        m = sea[at, :].astype(F32)
        wet[at, pl.ds(0, COLS)] = m
        for l in range(LEVELS):
            field[l, at, pl.ds(0, COLS)] = mem[l, at, :] * inc[l, at, :] * m
        first = jnp.zeros((8, 128), F32)
        last = jnp.zeros((8, 128), F32)
        left = [field[l, at, pl.ds(0, 128)] for l in range(LEVELS)]
        left += [zon[at, pl.ds(0, 128)], mer[at, pl.ds(0, 128)], m[:, :128]]
        right = [field[l, at, pl.ds(COLS - 128, 128)] for l in range(LEVELS)]
        right += [zon[at, pl.ds(COLS - 128, 128)], mer[at, pl.ds(COLS - 128, 128)], m[:, COLS - 128:]]
        for f in range(7):
            here = (lane >= 4 * f) & (lane < 4 * f + 4)
            a = left[f] if f == 0 else pltpu.roll(left[f], 4 * f, 1)
            b = pltpu.roll(right[f], 4 * f + 4, 1)
            first = jnp.where(here, a, first)
            last = jnp.where(here, b, last)
        cols_out[0, at, :] = first
        cols_out[1, at, :] = last
        return carry

    lax.fori_loop(0, 8, start_tile, 0)

    def tables(at):
        both = [field[l, at, pl.ds(0, COLS)] for l in range(LEVELS)]
        return both + [zon[at, :], mer[at, :], wet[at, pl.ds(0, COLS)]]

    top = tables(pl.ds(0, 8))
    bottom = tables(pl.ds(ROWS - 8, 8))
    for i in range(4):
        if i < 3:
            rows_out[0, i] = jnp.where(low, top[2 * i], pltpu.roll(top[2 * i + 1], 4, 0))
            rows_out[1, i] = jnp.where(low, pltpu.roll(bottom[2 * i + 1], 4, 0), bottom[2 * i])
        else:
            rows_out[0, i] = top[6]
            rows_out[1, i] = bottom[6]

    pl.semaphore_wait(barrier, len(partners))

    def push(src, dst, send, recv, device):
        return pltpu.make_async_remote_copy(
            src_ref=src, dst_ref=dst, send_sem=send, recv_sem=recv,
            device_id=device, device_id_type=MESH,
        )

    halo = [
        push(rows_out.at[0], rows_in.at[0], halo_send.at[0], halo_recv.at[0], beside(-1, 0)),
        push(rows_out.at[1], rows_in.at[1], halo_send.at[1], halo_recv.at[1], beside(1, 0)),
        push(cols_out.at[0], cols_in.at[0], halo_send.at[2], halo_recv.at[2], beside(0, -1)),
        push(cols_out.at[1], cols_in.at[1], halo_send.at[3], halo_recv.at[3], beside(0, 1)),
    ]
    for side in range(2):
        for end in range(2):
            i = side * 2 + end
            halo.append(
                push(
                    cols_out.at[side, pl.ds(end * (ROWS - 8), 8)],
                    corner_in.at[side, end],
                    halo_send.at[4 + i], halo_recv.at[4 + i],
                    beside(-1 if end == 0 else 1, -1 if side == 0 else 1),
                )
            )
    for copy in halo:
        copy.start()
    for copy in halo:
        copy.wait_recv()

    has_after = gy < 3
    has_before = gy > 0
    edge_ok = jnp.where(low, has_after.astype(jnp.int32), has_before.astype(jnp.int32)) > 0

    after_before = []
    for i in range(4):
        n, s = rows_in[0, i], rows_in[1, i]
        after_before.append(jnp.where(edge_ok, jnp.where(low, n, s), 0.0))
        if i < 3:
            swap = pltpu.roll(jnp.where(low, s, n), 4, 0)
            after_before.append(jnp.where(edge_ok, swap, 0.0))
    tail = pl.ds(ROWS, 8)
    for l in range(LEVELS):
        field[l, tail, pl.ds(0, COLS)] = after_before[l]
    wet[tail, pl.ds(0, COLS)] = after_before[6]

    def side_tile(f, right, left):
        a = right if f == 0 else pltpu.roll(right, 128 - 4 * f, 1)
        b = pltpu.roll(left, 124 - 4 * f, 1)
        return jnp.where(lane < 4, a, jnp.where(lane >= 124, b, 0.0))

    def columns(r, carry):
        at = pl.ds(pl.multiple_of(r * 8, 8), 8)
        right, left = cols_in[0, at, :], cols_in[1, at, :]
        for l in range(LEVELS):
            field[l, at, pl.ds(COLS, 128)] = side_tile(l, right, left)
        east[at, pl.ds(COLS, 128)] = side_tile(4, right, left)
        north[at, pl.ds(COLS, 128)] = side_tile(5, right, left)
        wet[at, pl.ds(COLS, 128)] = side_tile(6, right, left)
        east[at, pl.ds(0, COLS)] = zon[at, :]
        north[at, pl.ds(0, COLS)] = mer[at, :]
        return carry

    lax.fori_loop(0, 8, columns, 0)
    right = jnp.where(edge_ok, jnp.where(low, corner_in[0, 0], corner_in[0, 1]), 0.0)
    left = jnp.where(edge_ok, jnp.where(low, corner_in[1, 0], corner_in[1, 1]), 0.0)
    for l in range(LEVELS):
        field[l, tail, pl.ds(COLS, 128)] = side_tile(l, right, left)
    east[tail, pl.ds(COLS, 128)] = side_tile(4, right, left)
    north[tail, pl.ds(COLS, 128)] = side_tile(5, right, left)
    wet[tail, pl.ds(COLS, 128)] = side_tile(6, right, left)
    east[tail, pl.ds(0, COLS)] = after_before[4]
    north[tail, pl.ds(0, COLS)] = after_before[5]

    wide = lax.broadcasted_iota(jnp.int32, (1, XCOLS), 1)
    inside = (wide < COLS + 3) | (wide >= XCOLS - 4)

    def rows_up(ref, r):
        here = pltpu.roll(ref[pl.ds(8 * r, 8), :], 7, 0)
        following = pltpu.roll(ref[pl.ds(8 * ((r + 1) % 9), 8), :], 7, 0)
        return jnp.where(sub == 7, following, here)

    for r in range(9):
        at = pl.ds(8 * r, 8)
        m = wet[at, :]
        east[at, :] = jnp.where(inside, east[at, :] * m * pltpu.roll(m, XCOLS - 1, 1), 0.0)
        weight = north[at, :] * m * rows_up(wet, r)
        if r == 8:
            weight = jnp.where(sub == 3, 0.0, weight)
        north[at, :] = weight

    def level(l, carry):
        for step in range(STEPS):
            src = field.at[l] if step % 2 == 0 else other
            dst = other if step % 2 == 0 else field.at[l]
            last_step = step == STEPS - 1

            def flux(r):
                return north[pl.ds(8 * r, 8), :] * (rows_up(src, r) - src[pl.ds(8 * r, 8), :])

            before = pltpu.roll(flux(8), 1, 0)
            for r in range(8 if last_step else 9):
                at = pl.ds(8 * r, 8)
                u = src[at, :]
                go_east = east[at, :] * (pltpu.roll(u, XCOLS - 1, 1) - u)
                go_west = pltpu.roll(go_east, 1, 1)
                go_north = flux(r)
                down = pltpu.roll(go_north, 1, 0)
                go_south = jnp.where(sub == 0, before, down)
                before = down
                new = u + go_east - go_west + go_north - go_south
                if last_step:
                    term[l, at, :] = mem[l, at, :] * new[:, :COLS]
                else:
                    dst[at, :] = new
        return carry

    my_half = pl.ds(pl.multiple_of(core * HALF, HALF), HALF)
    their_half = pl.ds(pl.multiple_of((1 - core) * HALF, HALF), HALF)
    my_rows = pl.ds(pl.multiple_of(z * 8, 8), 8)

    def core_copy(l):
        return push(term.at[l, :, their_half], peer.at[l], core_send.at[l], core_recv.at[l], core_peer)

    def reduce_copy(l, k):
        to = lax.rem(z + k, 8)
        rows = pl.ds(pl.multiple_of(to * 8, 8), 8)
        return push(part.at[l, rows], gathered.at[k - 1, l], red_send.at[k - 1, l], red_recv.at[k - 1, l], along(k))

    def y_copy(l):
        return push(mine.at[l], across.at[l], y_send.at[l], y_recv.at[l], y_peer)

    def gather_copy(l, k):
        piece = out.at[l, my_rows, my_half]
        return push(piece, piece, ag_send.at[k - 1, l], ag_recv.at[k - 1, l], along(k))

    def forward_copy(l, k):
        source = lax.rem(z + 8 - k, 8)
        piece = out.at[l, pl.ds(pl.multiple_of(source * 8, 8), 8), my_half]
        return push(piece, piece, fwd_send.at[k, l], fwd_recv.at[k, l], core_peer)

    def reduce_level(l):
        core_copy(l).wait_recv()
        part[l] = term[l, :, my_half] + peer[l]
        for k in range(1, 8):
            reduce_copy(l, k).start()

    def compute(l, carry):
        level(l, 0)
        core_copy(l).start()

        @pl.when(l > 0)
        def _():
            reduce_level(l - 1)

        return carry

    lax.fori_loop(0, LEVELS, compute, 0)
    reduce_level(LEVELS - 1)

    def sum_level(l, carry):
        total = part[l, my_rows, :]
        for k in range(1, 8):
            reduce_copy(l, k).wait_recv()
            total = total + gathered[k - 1, l]
        mine[l] = total
        y_copy(l).start()
        return carry

    lax.fori_loop(0, LEVELS, sum_level, 0)

    def share_level(l, carry):
        y_copy(l).wait_recv()
        out[l, my_rows, my_half] = mine[l] + across[l]
        for k in range(1, 8):
            gather_copy(l, k).start()
        forward_copy(l, 0).start()
        return carry

    lax.fori_loop(0, LEVELS, share_level, 0)

    def pass_level(l, carry):
        for k in range(1, 8):
            gather_copy(l, k).wait_recv()
            forward_copy(l, k).start()
        return carry

    lax.fori_loop(0, LEVELS, pass_level, 0)

    def drain(l, carry):
        for k in range(8):
            forward_copy(l, k).wait()
        for k in range(1, 8):
            gather_copy(l, k).wait_send()
            reduce_copy(l, k).wait_send()
        core_copy(l).wait_send()
        y_copy(l).wait_send()
        return carry

    lax.fori_loop(0, LEVELS, drain, 0)
    for copy in halo:
        copy.wait_send()


def shards(increment, members, zonal_diff, merid_diff, sea_mask):
    vmem = pltpu.VMEM
    dma = pltpu.SemaphoreType.DMA
    return pl.pallas_call(
        kernel,
        out_shape=jax.ShapeDtypeStruct((LEVELS, ROWS, COLS), F32),
        in_specs=[pl.BlockSpec(memory_space=pl.ANY)] * 5,
        out_specs=pl.BlockSpec(memory_space=pltpu.VMEM),
        scratch_shapes=[
            vmem((LEVELS, ROWS, COLS), F32),
            vmem((LEVELS, ROWS, COLS), F32),
            vmem((ROWS, COLS), F32),
            vmem((ROWS, COLS), F32),
            vmem((ROWS, COLS), jnp.int32),
            vmem((LEVELS, XROWS, XCOLS), F32),
            vmem((XROWS, XCOLS), F32),
            vmem((XROWS, XCOLS), F32),
            vmem((XROWS, XCOLS), F32),
            vmem((XROWS, XCOLS), F32),
            vmem((2, 4, 8, COLS), F32),
            vmem((2, 4, 8, COLS), F32),
            vmem((2, ROWS, 128), F32),
            vmem((2, ROWS, 128), F32),
            vmem((2, 2, 8, 128), F32),
            vmem((LEVELS, ROWS, COLS), F32),
            vmem((LEVELS, ROWS, HALF), F32),
            vmem((LEVELS, ROWS, HALF), F32),
            vmem((7, LEVELS, 8, HALF), F32),
            vmem((LEVELS, 8, HALF), F32),
            vmem((LEVELS, 8, HALF), F32),
            dma((5,)),
            dma((8,)), dma((8,)),
            dma((LEVELS,)), dma((LEVELS,)),
            dma((7, LEVELS)), dma((7, LEVELS)),
            dma((LEVELS,)), dma((LEVELS,)),
            dma((7, LEVELS)), dma((7, LEVELS)),
            dma((8, LEVELS)), dma((8, LEVELS)),
        ],
        compiler_params=pltpu.CompilerParams(collective_id=0, has_side_effects=True),
    )(increment, members, zonal_diff, merid_diff, sea_mask)


def solution(mesh):
    return jax.shard_map(
        shards,
        mesh=mesh,
        in_specs=(
            P(None, "gy", "gx"),
            P("mem", None, "gy", "gx"),
            P("gy", "gx"),
            P("gy", "gx"),
            P("gy", "gx"),
        ),
        out_specs=P(None, "gy", "gx"),
        check_vma=False,
    )
```

time: 462 us -> 60.4 us (0.13)
  waiting for transfers between devices: 377 us -> 0 us
  Pallas kernels: 0 us -> 57.9 us
  starting transfers between devices: 56.4 us -> 0 us
  between operations: 13.8 us -> 0.01 us
  other arithmetic: 8.6 us -> 0 us
    psum x1 -> x0, waiting for transfers between devices: 361 us -> none  [shards(): return lax.psum(term, 'mem')]
    pallas_call x0 -> x1, Pallas kernels: none -> 57.9 us  [shards(): pl.pallas_call(kernel, out_shape=jax.ShapeDtypeStruct((LEVELS, ROWS, COLS...]
    ppermute x20 -> x0, starting transfers between devices: 56.4 us -> none  [the longest x10 34.9 us: extended(): before = lax.ppermute(last, axis, up)]
    ppermute x20 -> x0, waiting for transfers between devices: 16.4 us -> none  [the longest x10 14.6 us: extended(): before = lax.ppermute(last, axis, up)]
  transfers between devices with their start and end apart: 21 -> 0, of which waited for: 11 -> 0; matrix products, arithmetic and copies ran while one was open for 1% -> 0% of each run, Pallas kernels for 0% -> 0%
where the time goes in v1:
time: 60.4 us; the launch traced here: 60.2 us
  Pallas kernels  57.9 us (96%)
  local copies, waits for them, and re-layouts  2.31 us (4%)
    pallas_call x1, Pallas kernels, shards(): pl.pallas_call(kernel, out_shape=jax.ShapeDtypeStruct((LEVELS, ROWS, COLS...  57.9 us
    unnamed x1, local copies, waits for them, and re-layouts  2.31 us

profile of v1, /device:TPU:1, one launch (start us, length us, event | category | flops | bytes accessed | tf_op | source)
XLA Modules:
  0.0 60.2 jit_solution(8219746972226933533)
XLA Ops:
  0.0 57.9 %shard_map.55 = f32[4,64,1024]{2,1,0:T(8,128)} custom-call(f32[4,64,1024]{2,1,0:T(8,128)} %inc_hbm.1, f32[1,4,64,1024]{3,2,1,0:T(8,128)} %mem_hbm.1, f32[64,1024]{1,0:T(8,128)} %zon_hbm.1, f32[64,1024]{1,0:T(8,128)} %mer_hbm.1, s32[64,1024]{1,0:T(8,128)} %sea_hbm.1), custom_call_target="tpu_custom_call" | custom-call | tf_op jit(solution)/shard_map/pallas_call | solution.py:316
  57.9 2.3 %copy.7 = f32[4,64,1024]{2,1,0:T(8,128)} copy(f32[4,64,1024]{2,1,0:T(8,128)} %shard_map.55) | data formatting | bytes 2097152

commit v2 on v1

--- a/solution.py
+++ b/solution.py
@@ -19,11 +19,11 @@
 def kernel(
     inc_hbm, mem_hbm, zon_hbm, mer_hbm, sea_hbm, out,
     inc, mem, zon, mer, sea,
-    field, other, wet, east, north,
+    field, other, wet, east, west, north, south,
     rows_out, rows_in, cols_out, cols_in, corner_in,
-    term, peer, part, gathered, mine, across,
+    term, peer, part, near, far, split, joint, joined, mine, across,
     load_sem, halo_send, halo_recv, core_send, core_recv,
-    red_send, red_recv, y_send, y_recv, ag_send, ag_recv, fwd_send, fwd_recv,
+    red_send, red_recv, join_send, join_recv, y_send, y_recv, ag_send, ag_recv, fwd_send, fwd_recv,
 ):
     me = lax.axis_index("mem")
     gy = lax.axis_index("gy")
@@ -40,7 +40,7 @@
         return (member_at(z, y // 4, core), lax.rem(y, 4), lax.rem(gx + dx + 4, 4))
 
     def along(k):
-        return (member_at(lax.rem(z + k, 8), hi, core), gy, gx)
+        return (member_at(lax.rem(z + k + 8, 8), hi, core), gy, gx)
 
     core_peer = (member_at(z, hi, 1 - core), gy, gx)
     y_peer = (member_at(z, 1 - hi, core), gy, gx)
@@ -188,14 +188,23 @@
         following = pltpu.roll(ref[pl.ds(8 * ((r + 1) % 9), 8), :], 7, 0)
         return jnp.where(sub == 7, following, here)
 
+    def rows_down(ref, r):
+        here = pltpu.roll(ref[pl.ds(8 * r, 8), :], 1, 0)
+        preceding = pltpu.roll(ref[pl.ds(8 * ((r + 8) % 9), 8), :], 1, 0)
+        return jnp.where(sub == 0, preceding, here)
+
     for r in range(9):
         at = pl.ds(8 * r, 8)
         m = wet[at, :]
-        east[at, :] = jnp.where(inside, east[at, :] * m * pltpu.roll(m, XCOLS - 1, 1), 0.0)
+        weight = jnp.where(inside, east[at, :] * m * pltpu.roll(m, XCOLS - 1, 1), 0.0)
+        east[at, :] = weight
+        west[at, :] = pltpu.roll(weight, 1, 1)
         weight = north[at, :] * m * rows_up(wet, r)
         if r == 8:
             weight = jnp.where(sub == 3, 0.0, weight)
         north[at, :] = weight
+    for r in range(9):
+        south[pl.ds(8 * r, 8), :] = rows_down(north, r)
 
     def level(l, carry):
         for step in range(STEPS):
@@ -203,19 +212,13 @@
             dst = other if step % 2 == 0 else field.at[l]
             last_step = step == STEPS - 1
 
-            def flux(r):
-                return north[pl.ds(8 * r, 8), :] * (rows_up(src, r) - src[pl.ds(8 * r, 8), :])
-
-            before = pltpu.roll(flux(8), 1, 0)
             for r in range(8 if last_step else 9):
                 at = pl.ds(8 * r, 8)
                 u = src[at, :]
                 go_east = east[at, :] * (pltpu.roll(u, XCOLS - 1, 1) - u)
-                go_west = pltpu.roll(go_east, 1, 1)
-                go_north = flux(r)
-                down = pltpu.roll(go_north, 1, 0)
-                go_south = jnp.where(sub == 0, before, down)
-                before = down
+                go_west = west[at, :] * (u - pltpu.roll(u, 1, 1))
+                go_north = north[at, :] * (rows_up(src, r) - u)
+                go_south = south[at, :] * (u - rows_down(src, r))
                 new = u + go_east - go_west + go_north - go_south
                 if last_step:
                     term[l, at, :] = mem[l, at, :] * new[:, :COLS]
@@ -230,10 +233,27 @@
     def core_copy(l):
         return push(term.at[l, :, their_half], peer.at[l], core_send.at[l], core_recv.at[l], core_peer)
 
-    def reduce_copy(l, k):
-        to = lax.rem(z + k, 8)
-        rows = pl.ds(pl.multiple_of(to * 8, 8), 8)
-        return push(part.at[l, rows], gathered.at[k - 1, l], red_send.at[k - 1, l], red_recv.at[k - 1, l], along(k))
+    def rows_of(k):
+        return pl.ds(pl.multiple_of(lax.rem(z + k + 8, 8) * 8, 8), 8)
+
+    def first_copies(l):
+        copies = []
+        for side, sign in enumerate((1, -1)):
+            cut = pl.ds(side * (HALF // 2), HALF // 2)
+            for i, (src, dst, to) in enumerate((
+                (part.at[l, rows_of(3 * sign)], far.at[side, l], sign),
+                (part.at[l, rows_of(4), cut], split.at[side, l], 2 * sign),
+                (part.at[l, rows_of(sign)], near.at[side, l], sign),
+            )):
+                at = side * 3 + i
+                copies.append(push(src, dst, red_send.at[at, l], red_recv.at[at, l], along(to)))
+        return copies
+
+    def second_copies(l):
+        return [
+            push(joint.at[side, l], joined.at[side, l], join_send.at[side, l], join_recv.at[side, l], along(2 * sign))
+            for side, sign in enumerate((1, -1))
+        ]
 
     def y_copy(l):
         return push(mine.at[l], across.at[l], y_send.at[l], y_recv.at[l], y_peer)
@@ -250,8 +270,8 @@
     def reduce_level(l):
         core_copy(l).wait_recv()
         part[l] = term[l, :, my_half] + peer[l]
-        for k in range(1, 8):
-            reduce_copy(l, k).start()
+        for copy in first_copies(l):
+            copy.start()
 
     def compute(l, carry):
         level(l, 0)
@@ -266,12 +286,28 @@
     lax.fori_loop(0, LEVELS, compute, 0)
     reduce_level(LEVELS - 1)
 
+    def join_level(l, carry):
+        first = first_copies(l)
+        second = second_copies(l)
+        for side, sign in enumerate((1, -1)):
+            first[side * 3].wait_recv()
+            first[side * 3 + 1].wait_recv()
+            joint[side, l] = part[l, rows_of(2 * sign), :] + far[side, l]
+            cut = pl.ds(side * (HALF // 2), HALF // 2)
+            joint[side, l, :, cut] = joint[side, l, :, cut] + split[side, l]
+            second[side].start()
+        return carry
+
+    lax.fori_loop(0, LEVELS, join_level, 0)
+
     def sum_level(l, carry):
-        total = part[l, my_rows, :]
-        for k in range(1, 8):
-            reduce_copy(l, k).wait_recv()
-            total = total + gathered[k - 1, l]
-        mine[l] = total
+        first = first_copies(l)
+        second = second_copies(l)
+        for side in range(2):
+            first[side * 3 + 2].wait_recv()
+            second[side].wait_recv()
+        total = part[l, my_rows, :] + near[0, l] + near[1, l]
+        mine[l] = total + joined[0, l] + joined[1, l]
         y_copy(l).start()
         return carry
 
@@ -280,9 +316,15 @@
     def share_level(l, carry):
         y_copy(l).wait_recv()
         out[l, my_rows, my_half] = mine[l] + across[l]
-        for k in range(1, 8):
-            gather_copy(l, k).start()
         forward_copy(l, 0).start()
+
+        def send(to, c):
+            @pl.when(to != z)
+            def _():
+                gather_copy(l, lax.rem(to - z + 8, 8)).start()
+            return c
+
+        lax.fori_loop(0, 8, send, 0)
         return carry
 
     lax.fori_loop(0, LEVELS, share_level, 0)
@@ -300,7 +342,8 @@
             forward_copy(l, k).wait()
         for k in range(1, 8):
             gather_copy(l, k).wait_send()
-            reduce_copy(l, k).wait_send()
+        for copy in first_copies(l) + second_copies(l):
+            copy.wait_send()
         core_copy(l).wait_send()
         y_copy(l).wait_send()
         return carry
@@ -315,7 +358,7 @@
     dma = pltpu.SemaphoreType.DMA
     return pl.pallas_call(
         kernel,
-        out_shape=jax.ShapeDtypeStruct((LEVELS, ROWS, COLS), F32),
+        out_shape=pltpu.VMEM((LEVELS, ROWS, COLS), F32),
         in_specs=[pl.BlockSpec(memory_space=pl.ANY)] * 5,
         out_specs=pl.BlockSpec(memory_space=pltpu.VMEM),
         scratch_shapes=[
@@ -329,6 +372,8 @@
             vmem((XROWS, XCOLS), F32),
             vmem((XROWS, XCOLS), F32),
             vmem((XROWS, XCOLS), F32),
+            vmem((XROWS, XCOLS), F32),
+            vmem((XROWS, XCOLS), F32),
             vmem((2, 4, 8, COLS), F32),
             vmem((2, 4, 8, COLS), F32),
             vmem((2, ROWS, 128), F32),
@@ -337,13 +382,18 @@
             vmem((LEVELS, ROWS, COLS), F32),
             vmem((LEVELS, ROWS, HALF), F32),
             vmem((LEVELS, ROWS, HALF), F32),
-            vmem((7, LEVELS, 8, HALF), F32),
+            vmem((2, LEVELS, 8, HALF), F32),
+            vmem((2, LEVELS, 8, HALF), F32),
+            vmem((2, LEVELS, 8, HALF // 2), F32),
+            vmem((2, LEVELS, 8, HALF), F32),
+            vmem((2, LEVELS, 8, HALF), F32),
             vmem((LEVELS, 8, HALF), F32),
             vmem((LEVELS, 8, HALF), F32),
             dma((5,)),
             dma((8,)), dma((8,)),
             dma((LEVELS,)), dma((LEVELS,)),
-            dma((7, LEVELS)), dma((7, LEVELS)),
+            dma((6, LEVELS)), dma((6, LEVELS)),
+            dma((2, LEVELS)), dma((2, LEVELS)),
             dma((LEVELS,)), dma((LEVELS,)),
             dma((7, LEVELS)), dma((7, LEVELS)),
             dma((8, LEVELS)), dma((8, LEVELS)),

time: 60.4 us -> 53.8 us (0.89)
  Pallas kernels: 57.9 us -> 52.7 us
  local copies, waits for them, and re-layouts: 2.31 us -> 0.97 us
    pallas_call x1, Pallas kernels: 57.9 us -> 52.7 us  [shards(): pl.pallas_call(kernel, out_shape=pltpu.VMEM((LEVELS, ROWS, COLS), F32), i...]
    unnamed x1, local copies, waits for them, and re-layouts: 2.31 us -> 0.97 us
where the time goes in v2:
time: 53.8 us; the launch traced here: 53.7 us
  Pallas kernels  52.7 us (98%)
  local copies, waits for them, and re-layouts  0.97 us (2%)
    pallas_call x1, Pallas kernels, shards(): pl.pallas_call(kernel, out_shape=pltpu.VMEM((LEVELS, ROWS, COLS), F32), i...  52.7 us

profile of v2, /device:TPU:1, one launch (start us, length us, event | category | flops | bytes accessed | tf_op | source)
XLA Modules:
  0.0 53.7 jit_solution(9521003822291124669)
XLA Ops:
  0.0 52.7 %shard_map.55 = f32[4,64,1024]{2,1,0:T(8,128)S(1)} custom-call(f32[4,64,1024]{2,1,0:T(8,128)} %inc_hbm.1, f32[1,4,64,1024]{3,2,1,0:T(8,128)} %mem_hbm.1, f32[64,1024]{1,0:T(8,128)} %zon_hbm.1, f32[64,1024]{1,0:T(8,128)} %mer_hbm.1, s32[64,1024]{1,0:T(8,128)} %sea_hbm.1), custom_call_target="tpu_custom_call" | custom-call | tf_op jit(solution)/shard_map/pallas_call | solution.py:359
  52.7 1.0 %copy.7 = f32[4,64,1024]{2,1,0:T(8,128)} copy(f32[4,64,1024]{2,1,0:T(8,128)S(1)} %shard_map.55) | data formatting | bytes 2097152

commit v3 on v2

--- a/solution.py
+++ b/solution.py
@@ -12,6 +12,8 @@
 XROWS = ROWS + 8
 XCOLS = COLS + 128
 HALF = COLS // 2
+EAGER = 0
+SOON = 2
 MESH = pl.DeviceIdType.MESH
 F32 = jnp.float32
 
@@ -23,7 +25,7 @@
     rows_out, rows_in, cols_out, cols_in, corner_in,
     term, peer, part, near, far, split, joint, joined, mine, across,
     load_sem, halo_send, halo_recv, core_send, core_recv,
-    red_send, red_recv, join_send, join_recv, y_send, y_recv, ag_send, ag_recv, fwd_send, fwd_recv,
+    red_send, red_recv, join_send, join_recv, y_send, y_recv, ag_send, ag_recv, relay_send, fwd_send, fwd_recv,
 ):
     me = lax.axis_index("mem")
     gy = lax.axis_index("gy")
@@ -131,7 +133,7 @@
                     beside(-1 if end == 0 else 1, -1 if side == 0 else 1),
                 )
             )
-    for copy in halo:
+    for copy in halo[::-1]:
         copy.start()
     for copy in halo:
         copy.wait_recv()
@@ -258,9 +260,63 @@
     def y_copy(l):
         return push(mine.at[l], across.at[l], y_send.at[l], y_recv.at[l], y_peer)
 
-    def gather_copy(l, k):
-        piece = out.at[l, my_rows, my_half]
-        return push(piece, piece, ag_send.at[k - 1, l], ag_recv.at[k - 1, l], along(k))
+    QUARTER = HALF // 2
+
+    def piece_of(l, source, part_):
+        start = core * HALF
+        if part_ is None:
+            where = pl.ds(pl.multiple_of(start, HALF), HALF)
+        else:
+            where = pl.ds(pl.multiple_of(start + part_ * QUARTER, QUARTER), QUARTER)
+        rows = pl.ds(pl.multiple_of(source * 8, 8), 8)
+        return out.at[l, rows, where]
+
+    def gather_copies(l, k):
+        if k == 4:
+            slots = [(3, 0), (7, 1)]
+        else:
+            slots = [(k - 1, None)]
+        copies = []
+        for slot, part_ in slots:
+            piece = piece_of(l, z, part_)
+            copies.append(push(piece, piece, ag_send.at[slot, l], ag_recv.at[slot, l], along(k)))
+        return copies
+
+    def soon(k):
+        return lax.rem(z + k + 8, 8) < SOON
+
+    def each_owned(l, act, early, late):
+        for k in range(1, 8):
+            def run(k=k):
+                for copy in gather_copies(l, k):
+                    act(copy)
+
+            if early:
+                pl.when(soon(k))(run)
+            if late and k in (1, 2, 6, 7):
+                pl.when(jnp.logical_not(soon(k)))(run)
+
+    def relay_copies(l, side):
+        sign = 1 - 2 * side
+        source = lax.rem(z - 2 * sign + 8, 8)
+        whole = piece_of(l, source, None)
+        half = piece_of(l, source, side)
+        slot = 2 if side == 0 else 4
+        half_slot = 3 if side == 0 else 7
+        return [
+            (sign, push(whole, whole, relay_send.at[2 * side, l], ag_recv.at[slot, l], along(sign))),
+            (2 * sign, push(half, half, relay_send.at[2 * side + 1, l], ag_recv.at[half_slot, l], along(2 * sign))),
+        ]
+
+    def each_relay(l, side, act):
+        for to, copy in relay_copies(l, side):
+            @pl.when(jnp.logical_not(soon(to)))
+            def _(copy=copy):
+                act(copy)
+
+    def arrived(l, k):
+        for copy in gather_copies(l, k):
+            copy.wait_recv()
 
     def forward_copy(l, k):
         source = lax.rem(z + 8 - k, 8)
@@ -316,32 +372,47 @@
     def share_level(l, carry):
         y_copy(l).wait_recv()
         out[l, my_rows, my_half] = mine[l] + across[l]
+        each_owned(l, lambda copy: copy.start(), True, False)
         forward_copy(l, 0).start()
 
-        def send(to, c):
-            @pl.when(to != z)
-            def _():
-                gather_copy(l, lax.rem(to - z + 8, 8)).start()
-            return c
-
-        lax.fori_loop(0, 8, send, 0)
+        @pl.when(l < EAGER)
+        def _():
+            each_owned(l, lambda copy: copy.start(), False, True)
+
+        return carry
+
+    def later_level(l, carry):
+        each_owned(l, lambda copy: copy.start(), False, True)
         return carry
 
     lax.fori_loop(0, LEVELS, share_level, 0)
+    lax.fori_loop(EAGER, LEVELS, later_level, 0)
 
     def pass_level(l, carry):
-        for k in range(1, 8):
-            gather_copy(l, k).wait_recv()
+        for side, k in enumerate((2, 6)):
+            arrived(l, k)
+            each_relay(l, side, lambda copy: copy.start())
             forward_copy(l, k).start()
+        for k in (1, 7):
+            arrived(l, k)
+            forward_copy(l, k).start()
+        return carry
+
+    def far_level(l, carry):
+        for k in (3, 5, 4):
+            arrived(l, k)
+            forward_copy(l, k).start()
         return carry
 
     lax.fori_loop(0, LEVELS, pass_level, 0)
+    lax.fori_loop(0, LEVELS, far_level, 0)
 
     def drain(l, carry):
         for k in range(8):
             forward_copy(l, k).wait()
-        for k in range(1, 8):
-            gather_copy(l, k).wait_send()
+        each_owned(l, lambda copy: copy.wait_send(), True, True)
+        for side in range(2):
+            each_relay(l, side, lambda copy: copy.wait_send())
         for copy in first_copies(l) + second_copies(l):
             copy.wait_send()
         core_copy(l).wait_send()
@@ -395,7 +466,8 @@
             dma((6, LEVELS)), dma((6, LEVELS)),
             dma((2, LEVELS)), dma((2, LEVELS)),
             dma((LEVELS,)), dma((LEVELS,)),
-            dma((7, LEVELS)), dma((7, LEVELS)),
+            dma((8, LEVELS)), dma((8, LEVELS)),
+            dma((4, LEVELS)),
             dma((8, LEVELS)), dma((8, LEVELS)),
         ],
         compiler_params=pltpu.CompilerParams(collective_id=0, has_side_effects=True),

time: 53.8 us -> 50.1 us (0.931)
  Pallas kernels: 52.7 us -> 49 us
    pallas_call x1, Pallas kernels: 52.7 us -> 49 us  [shards(): pl.pallas_call(kernel, out_shape=pltpu.VMEM((LEVELS, ROWS, COLS), F32), i...]
where the time goes in v3:
time: 50.1 us; the launch traced here: 50 us
  Pallas kernels  49 us (98%)
  local copies, waits for them, and re-layouts  0.97 us (2%)
    pallas_call x1, Pallas kernels, shards(): pl.pallas_call(kernel, out_shape=pltpu.VMEM((LEVELS, ROWS, COLS), F32), i...  49 us

profile of v3, /device:TPU:1, one launch (start us, length us, event | category | flops | bytes accessed | tf_op | source)
XLA Modules:
  0.0 50.0 jit_solution(7791124766363525997)
XLA Ops:
  0.0 49.0 %shard_map.55 = f32[4,64,1024]{2,1,0:T(8,128)S(1)} custom-call(f32[4,64,1024]{2,1,0:T(8,128)} %inc_hbm.1, f32[1,4,64,1024]{3,2,1,0:T(8,128)} %mem_hbm.1, f32[64,1024]{1,0:T(8,128)} %zon_hbm.1, f32[64,1024]{1,0:T(8,128)} %mer_hbm.1, s32[64,1024]{1,0:T(8,128)} %sea_hbm.1), custom_call_target="tpu_custom_call" | custom-call | tf_op jit(solution)/shard_map/pallas_call | solution.py:430
  49.0 1.0 %copy.7 = f32[4,64,1024]{2,1,0:T(8,128)} copy(f32[4,64,1024]{2,1,0:T(8,128)S(1)} %shard_map.55) | data formatting | bytes 2097152

commit v4 on v3

--- a/solution.py
+++ b/solution.py
@@ -21,7 +21,7 @@
 def kernel(
     inc_hbm, mem_hbm, zon_hbm, mer_hbm, sea_hbm, out,
     inc, mem, zon, mer, sea,
-    field, other, wet, east, west, north, south,
+    field, other, edge_cols, edge_rows, wet, east, west, north, south,
     rows_out, rows_in, cols_out, cols_in, corner_in,
     term, peer, part, near, far, split, joint, joined, mine, across,
     load_sem, halo_send, halo_recv, core_send, core_recv,
@@ -92,7 +92,7 @@
         cols_out[1, at, :] = last
         return carry
 
-    lax.fori_loop(0, 8, start_tile, 0)
+    lax.fori_loop(0, 8, start_tile, 0, unroll=True)
 
     def tables(at):
         both = [field[l, at, pl.ds(0, COLS)] for l in range(LEVELS)]
@@ -135,6 +135,53 @@
             )
     for copy in halo[::-1]:
         copy.start()
+    wide = lax.broadcasted_iota(jnp.int32, (1, XCOLS), 1)
+
+    def tile(r):
+        return pl.ds(8 * r, 8)
+
+    def shift_up(here, following):
+        return jnp.where(sub == 7, pltpu.roll(following, 7, 0), pltpu.roll(here, 7, 0))
+
+    def shift_down(here, preceding):
+        return jnp.where(sub == 0, pltpu.roll(preceding, 1, 0), pltpu.roll(here, 1, 0))
+
+    def stepped(u, above, below, weights):
+        n = u.shape[1]
+        to_east, to_west, to_north, to_south = weights
+        go_east = to_east * (pltpu.roll(u, n - 1, 1) - u)
+        go_west = to_west * (u - pltpu.roll(u, 1, 1))
+        go_north = to_north * (shift_up(u, above) - u)
+        go_south = to_south * (u - shift_down(u, below))
+        return u + go_east - go_west + go_north - go_south
+
+    own = pl.ds(0, COLS)
+    for r in range(8):
+        at = tile(r)
+        m = wet[at, own]
+        weight = zon[at, :] * m * pltpu.roll(m, COLS - 1, 1)
+        east[at, own] = weight
+        west[at, own] = pltpu.roll(weight, 1, 1)
+        north[at, own] = mer[at, :] * m * shift_up(m, wet[tile((r + 1) % 8), own])
+    for r in range(8):
+        south[tile(r), own] = shift_down(north[tile(r), own], north[tile((r + 7) % 8), own])
+
+    def alone(l, carry):
+        for step in range(STEPS):
+            src = field.at[l, :, own] if step == 0 else other.at[(step - 1) % 2, :, own]
+            dst = other.at[step % 2, :, own]
+            for r in range(8):
+                at = tile(r)
+                weights = [w[at, own] for w in (east, west, north, south)]
+                new = stepped(src[at, :], src[tile((r + 1) % 8), :], src[tile((r + 7) % 8), :], weights)
+                if step == STEPS - 1:
+                    term[l, at, :] = mem[l, at, :] * new
+                else:
+                    dst[at, :] = new
+        return carry
+
+    lax.fori_loop(0, LEVELS, alone, 0)
+
     for copy in halo:
         copy.wait_recv()
 
@@ -167,11 +214,9 @@
         east[at, pl.ds(COLS, 128)] = side_tile(4, right, left)
         north[at, pl.ds(COLS, 128)] = side_tile(5, right, left)
         wet[at, pl.ds(COLS, 128)] = side_tile(6, right, left)
-        east[at, pl.ds(0, COLS)] = zon[at, :]
-        north[at, pl.ds(0, COLS)] = mer[at, :]
-        return carry
-
-    lax.fori_loop(0, 8, columns, 0)
+        return carry
+
+    lax.fori_loop(0, 8, columns, 0, unroll=True)
     right = jnp.where(edge_ok, jnp.where(low, corner_in[0, 0], corner_in[0, 1]), 0.0)
     left = jnp.where(edge_ok, jnp.where(low, corner_in[1, 0], corner_in[1, 1]), 0.0)
     for l in range(LEVELS):
@@ -182,50 +227,72 @@
     east[tail, pl.ds(0, COLS)] = after_before[4]
     north[tail, pl.ds(0, COLS)] = after_before[5]
 
-    wide = lax.broadcasted_iota(jnp.int32, (1, XCOLS), 1)
     inside = (wide < COLS + 3) | (wide >= XCOLS - 4)
-
-    def rows_up(ref, r):
-        here = pltpu.roll(ref[pl.ds(8 * r, 8), :], 7, 0)
-        following = pltpu.roll(ref[pl.ds(8 * ((r + 1) % 9), 8), :], 7, 0)
-        return jnp.where(sub == 7, following, here)
-
-    def rows_down(ref, r):
-        here = pltpu.roll(ref[pl.ds(8 * r, 8), :], 1, 0)
-        preceding = pltpu.roll(ref[pl.ds(8 * ((r + 8) % 9), 8), :], 1, 0)
-        return jnp.where(sub == 0, preceding, here)
-
-    for r in range(9):
-        at = pl.ds(8 * r, 8)
-        m = wet[at, :]
-        weight = jnp.where(inside, east[at, :] * m * pltpu.roll(m, XCOLS - 1, 1), 0.0)
-        east[at, :] = weight
-        west[at, :] = pltpu.roll(weight, 1, 1)
-        weight = north[at, :] * m * rows_up(wet, r)
-        if r == 8:
-            weight = jnp.where(sub == 3, 0.0, weight)
-        north[at, :] = weight
-    for r in range(9):
-        south[pl.ds(8 * r, 8), :] = rows_down(north, r)
+    side = pl.ds(COLS - 128, 256)
+    inside3 = jnp.concatenate([inside[:, COLS - 128:], inside[:, :128]], axis=1)
+
+    def ring(ref, at):
+        return jnp.concatenate([ref[at, side], ref[at, pl.ds(0, 128)]], axis=1)
+
+    for r in range(8):
+        at = tile(r)
+        m = ring(wet, at)
+        z3 = jnp.concatenate([zon[at, pl.ds(COLS - 128, 128)], east[at, pl.ds(COLS, 128)], zon[at, pl.ds(0, 128)]], axis=1)
+        weight = jnp.where(inside3, z3 * m * pltpu.roll(m, 383, 1), 0.0)
+        east[at, side] = weight[:, :256]
+        back = pltpu.roll(weight, 1, 1)
+        west[at, pl.ds(COLS, 128)] = back[:, 128:256]
+        west[at, pl.ds(0, 128)] = back[:, 256:]
+    m = wet[tail, :]
+    weight = jnp.where(inside, east[tail, :] * m * pltpu.roll(m, XCOLS - 1, 1), 0.0)
+    east[tail, :] = weight
+    west[tail, :] = pltpu.roll(weight, 1, 1)
+    halo_cols = pl.ds(COLS, 128)
+    for r in range(7):
+        up = shift_up(wet[tile(r), halo_cols], wet[tile(r + 1), halo_cols])
+        north[tile(r), halo_cols] = north[tile(r), halo_cols] * wet[tile(r), halo_cols] * up
+    edge = tile(7)
+    merid = jnp.concatenate([mer[edge, :], north[edge, halo_cols]], axis=1)
+    north[edge, :] = merid * wet[edge, :] * shift_up(wet[edge, :], m)
+    weight = north[tail, :] * m * shift_up(m, wet[tile(0), :])
+    north[tail, :] = jnp.where(sub == 3, 0.0, weight)
+    for r in range(1, 8):
+        south[tile(r), halo_cols] = shift_down(north[tile(r), halo_cols], north[tile(r - 1), halo_cols])
+    south[tail, :] = shift_down(north[tail, :], north[edge, :])
+    south[tile(0), :] = shift_down(north[tile(0), :], north[tail, :])
 
     def level(l, carry):
         for step in range(STEPS):
-            src = field.at[l] if step % 2 == 0 else other
-            dst = other if step % 2 == 0 else field.at[l]
-            last_step = step == STEPS - 1
-
-            for r in range(8 if last_step else 9):
-                at = pl.ds(8 * r, 8)
-                u = src[at, :]
-                go_east = east[at, :] * (pltpu.roll(u, XCOLS - 1, 1) - u)
-                go_west = west[at, :] * (u - pltpu.roll(u, 1, 1))
-                go_north = north[at, :] * (rows_up(src, r) - u)
-                go_south = south[at, :] * (u - rows_down(src, r))
-                new = u + go_east - go_west + go_north - go_south
-                if last_step:
-                    term[l, at, :] = mem[l, at, :] * new[:, :COLS]
+            for r in range(8):
+                at = tile(r)
+                if step == 0:
+                    u, a, b = (ring(field.at[l], tile(i % 8)) for i in (r, r + 1, r + 7))
                 else:
-                    dst[at, :] = new
+                    src = edge_cols.at[(step - 1) % 2]
+                    u, a, b = (src[tile(i % 8), :] for i in (r, r + 1, r + 7))
+                new = stepped(u, a, b, [ring(w, at) for w in (east, west, north, south)])
+                if step < STEPS - 1:
+                    edge_cols[step % 2, at, :] = new
+                    continue
+                for lanes, part_, here in ((pl.ds(COLS - 128, 128), new[:, :128], lane >= 124), (pl.ds(0, 128), new[:, 256:], lane < 4)):
+                    term[l, at, lanes] = jnp.where(here, mem[l, at, lanes] * part_, term[l, at, lanes])
+        order = (7, 8, 0)
+        for step in range(STEPS):
+            for i, r in enumerate(order):
+                if step == STEPS - 1 and r == 8:
+                    continue
+                if step == 0:
+                    u, a, b = (field[l, tile(order[k % 3]), :] for k in (i, i + 1, i + 2))
+                else:
+                    src = edge_rows.at[(step - 1) % 2]
+                    u, a, b = (src[tile(k % 3), :] for k in (i, i + 1, i + 2))
+                new = stepped(u, a, b, [w[tile(r), :] for w in (east, west, north, south)])
+                if step < STEPS - 1:
+                    edge_rows[step % 2, tile(i), :] = new
+                    continue
+                at = tile(r)
+                here = low if r == 0 else jnp.logical_not(low)
+                term[l, at, :] = jnp.where(here, mem[l, at, :] * new[:, :COLS], term[l, at, :])
         return carry
 
     my_half = pl.ds(pl.multiple_of(core * HALF, HALF), HALF)
@@ -326,8 +393,9 @@
     def reduce_level(l):
         core_copy(l).wait_recv()
         part[l] = term[l, :, my_half] + peer[l]
-        for copy in first_copies(l):
-            copy.start()
+        first = first_copies(l)
+        for i in (0, 3, 1, 4):
+            first[i].start()
 
     def compute(l, carry):
         level(l, 0)
@@ -352,6 +420,8 @@
             cut = pl.ds(side * (HALF // 2), HALF // 2)
             joint[side, l, :, cut] = joint[side, l, :, cut] + split[side, l]
             second[side].start()
+        for side in range(2):
+            first[side * 3 + 2].start()
         return carry
 
     lax.fori_loop(0, LEVELS, join_level, 0)
@@ -439,7 +509,9 @@
             vmem((ROWS, COLS), F32),
             vmem((ROWS, COLS), jnp.int32),
             vmem((LEVELS, XROWS, XCOLS), F32),
-            vmem((XROWS, XCOLS), F32),
+            vmem((2, ROWS, COLS), F32),
+            vmem((2, ROWS, 384), F32),
+            vmem((2, 24, XCOLS), F32),
             vmem((XROWS, XCOLS), F32),
             vmem((XROWS, XCOLS), F32),
             vmem((XROWS, XCOLS), F32),

time: 50.1 us -> 49.3 us (0.984)
  Pallas kernels: 49 us -> 48.2 us
    pallas_call x1, Pallas kernels: 49 us -> 48.2 us  [shards(): pl.pallas_call(kernel, out_shape=pltpu.VMEM((LEVELS, ROWS, COLS), F32), i...]
where the time goes in v4:
time: 49.3 us; the launch traced here: 49.1 us
  Pallas kernels  48.2 us (98%)
  local copies, waits for them, and re-layouts  0.97 us (2%)
    pallas_call x1, Pallas kernels, shards(): pl.pallas_call(kernel, out_shape=pltpu.VMEM((LEVELS, ROWS, COLS), F32), i...  48.2 us

profile of v4, /device:TPU:1, one launch (start us, length us, event | category | flops | bytes accessed | tf_op | source)
XLA Modules:
  0.0 49.1 jit_solution(6774160002167110086)
XLA Ops:
  0.0 48.2 %shard_map.55 = f32[4,64,1024]{2,1,0:T(8,128)S(1)} custom-call(f32[4,64,1024]{2,1,0:T(8,128)} %inc_hbm.1, f32[1,4,64,1024]{3,2,1,0:T(8,128)} %mem_hbm.1, f32[64,1024]{1,0:T(8,128)} %zon_hbm.1, f32[64,1024]{1,0:T(8,128)} %mer_hbm.1, s32[64,1024]{1,0:T(8,128)} %sea_hbm.1), custom_call_target="tpu_custom_call" | custom-call | tf_op jit(solution)/shard_map/pallas_call | solution.py:500
  48.2 1.0 %copy.7 = f32[4,64,1024]{2,1,0:T(8,128)} copy(f32[4,64,1024]{2,1,0:T(8,128)S(1)} %shard_map.55) | data formatting | bytes 2097152

commit v5 on v4

--- a/solution.py
+++ b/solution.py
@@ -458,6 +458,15 @@
     lax.fori_loop(0, LEVELS, share_level, 0)
     lax.fori_loop(EAGER, LEVELS, later_level, 0)
 
+    def far_pieces(l):
+        for k in (3, 5, 4):
+            arrived(l, k)
+            forward_copy(l, k).start()
+
+    def far_level(l, carry):
+        pl.when(z >= SOON)(lambda: far_pieces(l))
+        return carry
+
     def pass_level(l, carry):
         for side, k in enumerate((2, 6)):
             arrived(l, k)
@@ -466,12 +475,7 @@
         for k in (1, 7):
             arrived(l, k)
             forward_copy(l, k).start()
-        return carry
-
-    def far_level(l, carry):
-        for k in (3, 5, 4):
-            arrived(l, k)
-            forward_copy(l, k).start()
+        pl.when(z < SOON)(lambda: far_pieces(l))
         return carry
 
     lax.fori_loop(0, LEVELS, pass_level, 0)

time: 49.3 us -> 49.1 us (level)
  no operation moved by 1% of the time
where the time goes in v5:
time: 49.1 us; the launch traced here: 48.9 us
  Pallas kernels  48 us (98%)
  local copies, waits for them, and re-layouts  0.97 us (2%)
    pallas_call x1, Pallas kernels, shards(): pl.pallas_call(kernel, out_shape=pltpu.VMEM((LEVELS, ROWS, COLS), F32), i...  48 us

profile of v5, /device:TPU:1, one launch (start us, length us, event | category | flops | bytes accessed | tf_op | source)
XLA Modules:
  0.0 48.9 jit_solution(2250453048925980725)
XLA Ops:
  0.0 48.0 %shard_map.55 = f32[4,64,1024]{2,1,0:T(8,128)S(1)} custom-call(f32[4,64,1024]{2,1,0:T(8,128)} %inc_hbm.1, f32[1,4,64,1024]{3,2,1,0:T(8,128)} %mem_hbm.1, f32[64,1024]{1,0:T(8,128)} %zon_hbm.1, f32[64,1024]{1,0:T(8,128)} %mer_hbm.1, s32[64,1024]{1,0:T(8,128)} %sea_hbm.1), custom_call_target="tpu_custom_call" | custom-call | tf_op jit(solution)/shard_map/pallas_call | solution.py:504
  48.0 1.0 %copy.7 = f32[4,64,1024]{2,1,0:T(8,128)} copy(f32[4,64,1024]{2,1,0:T(8,128)S(1)} %shard_map.55) | data formatting | bytes 2097152

commit v6 on v5

--- a/solution.py
+++ b/solution.py
@@ -182,50 +182,23 @@
 
     lax.fori_loop(0, LEVELS, alone, 0)
 
-    for copy in halo:
+    for copy in halo[2:4]:
         copy.wait_recv()
-
-    has_after = gy < 3
-    has_before = gy > 0
-    edge_ok = jnp.where(low, has_after.astype(jnp.int32), has_before.astype(jnp.int32)) > 0
-
-    after_before = []
-    for i in range(4):
-        n, s = rows_in[0, i], rows_in[1, i]
-        after_before.append(jnp.where(edge_ok, jnp.where(low, n, s), 0.0))
-        if i < 3:
-            swap = pltpu.roll(jnp.where(low, s, n), 4, 0)
-            after_before.append(jnp.where(edge_ok, swap, 0.0))
-    tail = pl.ds(ROWS, 8)
-    for l in range(LEVELS):
-        field[l, tail, pl.ds(0, COLS)] = after_before[l]
-    wet[tail, pl.ds(0, COLS)] = after_before[6]
 
     def side_tile(f, right, left):
         a = right if f == 0 else pltpu.roll(right, 128 - 4 * f, 1)
         b = pltpu.roll(left, 124 - 4 * f, 1)
         return jnp.where(lane < 4, a, jnp.where(lane >= 124, b, 0.0))
 
-    def columns(r, carry):
-        at = pl.ds(pl.multiple_of(r * 8, 8), 8)
+    halo_cols = pl.ds(COLS, 128)
+    for r in range(8):
+        at = tile(r)
         right, left = cols_in[0, at, :], cols_in[1, at, :]
         for l in range(LEVELS):
-            field[l, at, pl.ds(COLS, 128)] = side_tile(l, right, left)
-        east[at, pl.ds(COLS, 128)] = side_tile(4, right, left)
-        north[at, pl.ds(COLS, 128)] = side_tile(5, right, left)
-        wet[at, pl.ds(COLS, 128)] = side_tile(6, right, left)
-        return carry
-
-    lax.fori_loop(0, 8, columns, 0, unroll=True)
-    right = jnp.where(edge_ok, jnp.where(low, corner_in[0, 0], corner_in[0, 1]), 0.0)
-    left = jnp.where(edge_ok, jnp.where(low, corner_in[1, 0], corner_in[1, 1]), 0.0)
-    for l in range(LEVELS):
-        field[l, tail, pl.ds(COLS, 128)] = side_tile(l, right, left)
-    east[tail, pl.ds(COLS, 128)] = side_tile(4, right, left)
-    north[tail, pl.ds(COLS, 128)] = side_tile(5, right, left)
-    wet[tail, pl.ds(COLS, 128)] = side_tile(6, right, left)
-    east[tail, pl.ds(0, COLS)] = after_before[4]
-    north[tail, pl.ds(0, COLS)] = after_before[5]
+            field[l, at, halo_cols] = side_tile(l, right, left)
+        east[at, halo_cols] = side_tile(4, right, left)
+        north[at, halo_cols] = side_tile(5, right, left)
+        wet[at, halo_cols] = side_tile(6, right, left)
 
     inside = (wide < COLS + 3) | (wide >= XCOLS - 4)
     side = pl.ds(COLS - 128, 256)
@@ -237,31 +210,18 @@
     for r in range(8):
         at = tile(r)
         m = ring(wet, at)
-        z3 = jnp.concatenate([zon[at, pl.ds(COLS - 128, 128)], east[at, pl.ds(COLS, 128)], zon[at, pl.ds(0, 128)]], axis=1)
+        z3 = jnp.concatenate([zon[at, pl.ds(COLS - 128, 128)], east[at, halo_cols], zon[at, pl.ds(0, 128)]], axis=1)
         weight = jnp.where(inside3, z3 * m * pltpu.roll(m, 383, 1), 0.0)
         east[at, side] = weight[:, :256]
         back = pltpu.roll(weight, 1, 1)
-        west[at, pl.ds(COLS, 128)] = back[:, 128:256]
+        west[at, halo_cols] = back[:, 128:256]
         west[at, pl.ds(0, 128)] = back[:, 256:]
-    m = wet[tail, :]
-    weight = jnp.where(inside, east[tail, :] * m * pltpu.roll(m, XCOLS - 1, 1), 0.0)
-    east[tail, :] = weight
-    west[tail, :] = pltpu.roll(weight, 1, 1)
-    halo_cols = pl.ds(COLS, 128)
-    for r in range(7):
-        up = shift_up(wet[tile(r), halo_cols], wet[tile(r + 1), halo_cols])
-        north[tile(r), halo_cols] = north[tile(r), halo_cols] * wet[tile(r), halo_cols] * up
-    edge = tile(7)
-    merid = jnp.concatenate([mer[edge, :], north[edge, halo_cols]], axis=1)
-    north[edge, :] = merid * wet[edge, :] * shift_up(wet[edge, :], m)
-    weight = north[tail, :] * m * shift_up(m, wet[tile(0), :])
-    north[tail, :] = jnp.where(sub == 3, 0.0, weight)
-    for r in range(1, 8):
-        south[tile(r), halo_cols] = shift_down(north[tile(r), halo_cols], north[tile(r - 1), halo_cols])
-    south[tail, :] = shift_down(north[tail, :], north[edge, :])
-    south[tile(0), :] = shift_down(north[tile(0), :], north[tail, :])
-
-    def level(l, carry):
+        up = shift_up(m[:, 128:256], wet[tile((r + 1) % 8), halo_cols])
+        north[at, halo_cols] = north[at, halo_cols] * m[:, 128:256] * up
+    for r in range(8):
+        south[tile(r), halo_cols] = shift_down(north[tile(r), halo_cols], north[tile((r + 7) % 8), halo_cols])
+
+    def near_cols(l, carry):
         for step in range(STEPS):
             for r in range(8):
                 at = tile(r)
@@ -276,6 +236,47 @@
                     continue
                 for lanes, part_, here in ((pl.ds(COLS - 128, 128), new[:, :128], lane >= 124), (pl.ds(0, 128), new[:, 256:], lane < 4)):
                     term[l, at, lanes] = jnp.where(here, mem[l, at, lanes] * part_, term[l, at, lanes])
+        return carry
+
+    lax.fori_loop(0, LEVELS, near_cols, 0)
+
+    for copy in halo[:2] + halo[4:]:
+        copy.wait_recv()
+
+    has_after = gy < 3
+    has_before = gy > 0
+    edge_ok = jnp.where(low, has_after.astype(jnp.int32), has_before.astype(jnp.int32)) > 0
+
+    after_before = []
+    for i in range(4):
+        n, s = rows_in[0, i], rows_in[1, i]
+        after_before.append(jnp.where(edge_ok, jnp.where(low, n, s), 0.0))
+        if i < 3:
+            swap = pltpu.roll(jnp.where(low, s, n), 4, 0)
+            after_before.append(jnp.where(edge_ok, swap, 0.0))
+    tail = pl.ds(ROWS, 8)
+    right = jnp.where(edge_ok, jnp.where(low, corner_in[0, 0], corner_in[0, 1]), 0.0)
+    left = jnp.where(edge_ok, jnp.where(low, corner_in[1, 0], corner_in[1, 1]), 0.0)
+    for l in range(LEVELS):
+        field[l, tail, own] = after_before[l]
+        field[l, tail, halo_cols] = side_tile(l, right, left)
+    zonal = jnp.concatenate([after_before[4], side_tile(4, right, left)], axis=1)
+    merid = jnp.concatenate([after_before[5], side_tile(5, right, left)], axis=1)
+    m = jnp.concatenate([after_before[6], side_tile(6, right, left)], axis=1)
+    weight = jnp.where(inside, zonal * m * pltpu.roll(m, XCOLS - 1, 1), 0.0)
+    east[tail, :] = weight
+    west[tail, :] = pltpu.roll(weight, 1, 1)
+    edge = tile(7)
+    edge_side = side_tile(5, cols_in[0, edge, :], cols_in[1, edge, :])
+    edge_merid = jnp.concatenate([mer[edge, :], edge_side], axis=1)
+    last = edge_merid * wet[edge, :] * shift_up(wet[edge, :], m)
+    north[edge, :] = last
+    beyond = jnp.where(sub == 3, 0.0, merid * m * shift_up(m, wet[tile(0), :]))
+    north[tail, :] = beyond
+    south[tail, :] = shift_down(beyond, last)
+    south[tile(0), :] = shift_down(north[tile(0), :], beyond)
+
+    def level(l, carry):
         order = (7, 8, 0)
         for step in range(STEPS):
             for i, r in enumerate(order):
@@ -400,15 +401,15 @@
     def compute(l, carry):
         level(l, 0)
         core_copy(l).start()
-
-        @pl.when(l > 0)
-        def _():
-            reduce_level(l - 1)
-
         return carry
 
     lax.fori_loop(0, LEVELS, compute, 0)
-    reduce_level(LEVELS - 1)
+
+    def reduce_all(l, carry):
+        reduce_level(l)
+        return carry
+
+    lax.fori_loop(0, LEVELS, reduce_all, 0)
 
     def join_level(l, carry):
         first = first_copies(l)

time: 49.1 us -> 49.4 us (level)
  no operation moved by 1% of the time
where the time goes in v6:
time: 49.4 us; the launch traced here: 48.9 us
  Pallas kernels  47.9 us (97%)
  local copies, waits for them, and re-layouts  0.97 us (2%)
    pallas_call x1, Pallas kernels, shards(): pl.pallas_call(kernel, out_shape=pltpu.VMEM((LEVELS, ROWS, COLS), F32), i...  47.9 us

profile of v6, /device:TPU:1, one launch (start us, length us, event | category | flops | bytes accessed | tf_op | source)
XLA Modules:
  0.0 48.9 jit_solution(121258844728896681)
XLA Ops:
  0.0 47.9 %shard_map.55 = f32[4,64,1024]{2,1,0:T(8,128)S(1)} custom-call(f32[4,64,1024]{2,1,0:T(8,128)} %inc_hbm.1, f32[1,4,64,1024]{3,2,1,0:T(8,128)} %mem_hbm.1, f32[64,1024]{1,0:T(8,128)} %zon_hbm.1, f32[64,1024]{1,0:T(8,128)} %mer_hbm.1, s32[64,1024]{1,0:T(8,128)} %sea_hbm.1), custom_call_target="tpu_custom_call" | custom-call | tf_op jit(solution)/shard_map/pallas_call | solution.py:505
  47.9 1.0 %copy.7 = f32[4,64,1024]{2,1,0:T(8,128)} copy(f32[4,64,1024]{2,1,0:T(8,128)S(1)} %shard_map.55) | data formatting | bytes 2097152
